TPU v7x, 128 devices: a whole 4x4x4 slice. The times are simulated.
128 devices in a mesh: space: 16 (over y, x), vel: 8 (over z, core).
Axes of the slice: x: 4, y: 4, z: 4, core: 2. Of those that a mesh axis runs over, the one named last changes fastest.
Arguments:
- space_factor: float32 [32, 64, 16, 128], P(None, 'space'), may hold values from -16 to 16
- core_matrix: float32 [32, 32], replicated, may hold values from -0.5 to 3
- velocity_factor: float32 [32, 110592], P(None, 'vel'), may hold values from -5 to 5
- collision_rates: float32 [64, 16, 128], P('space'), may hold values from 0.05 to 0.5
Outputs:
- space_next: float32 [32, 64, 16, 128], P(None, 'space')
- core_next: float32 [32, 32], replicated
- velocity_next: float32 [32, 110592], P(None, 'vel')
All inputs are finite; a program needn't handle non-finite values.
Results may differ from a plain program's by a relative error of at most 0.0003.
Values sent between devices are 32-bit elements; how exact they have to be, the bound alone decides.
No kernel may reach another device: no remote copies, remote signals or barrier semaphores. Data moves between devices by JAX's collectives and lax.ppermute only.
A program may use at most 128 MiB of HBM per device.

v0:
```python
import jax
import jax.numpy as jnp
from jax import lax
from jax.sharding import PartitionSpec as P

NVD = 48
SUB = 3
highest = lax.Precision.HIGHEST
velocity_extent = 0.25
thermal_speed = 0.125
time_step = 1.0


def from_behind(block, axis, distance):
    devices = range(lax.axis_size(axis))
    route = [((i - distance) % len(devices), i) for i in devices]
    return lax.ppermute(block, axis, route)


def padded_2(cells, sides, width):
    for axis, dim in sides:
        count = lax.axis_size(axis)
        head = lax.slice_in_dim(cells, 0, width, axis=dim)
        tail = lax.slice_in_dim(cells, cells.shape[dim] - width, cells.shape[dim], axis=dim)
        cells = jnp.concatenate(
            [
                lax.ppermute(tail, axis, [(i, (i + 1) % count) for i in range(count)]),
                cells,
                lax.ppermute(head, axis, [((i + 1) % count, i) for i in range(count)]),
            ],
            axis=dim,
        )
    return cells


def velocity_grid(first_point, length):
    points = first_point + jnp.arange(length, dtype=jnp.int32)
    digits = [points // (NVD * NVD), points // NVD % NVD, points % NVD]
    components = [
        velocity_extent * ((2 * numeral + 1).astype(jnp.float32) / NVD - 1.0) for numeral in digits
    ]
    axis_points = velocity_extent * (
        (2 * jnp.arange(NVD, dtype=jnp.int32) + 1).astype(jnp.float32) / NVD - 1.0
    )
    twice_variance = 2.0 * thermal_speed * thermal_speed
    line_mean = jnp.mean(jnp.exp(-axis_points * axis_points / twice_variance))
    squared_speed = (
        components[0] * components[0]
        + components[1] * components[1]
        + components[2] * components[2]
    )
    profile = jnp.exp(-squared_speed / twice_variance) / (line_mean * line_mean * line_mean)
    return (jnp.stack(components), profile)


def products(leading, others, divisor):
    return lax.dot_general(leading, others, (((1,), (1,)), ((), ())), precision=highest) / divisor


def flatten_rows(values):
    return values.reshape(values.shape[0], -1)


def apply_rows(matrix, values):
    return jnp.dot(matrix, flatten_rows(values), precision=highest).reshape(
        (matrix.shape[0],) + values.shape[1:]
    )


def triangular_inverse(gram_matrix):
    factor = jnp.linalg.cholesky(gram_matrix)
    identity = jnp.eye(gram_matrix.shape[0], dtype=gram_matrix.dtype)
    return jax.scipy.linalg.solve_triangular(factor, identity, lower=True)


def lower_differences(values, lower_plane):
    shifted = jnp.concatenate([lower_plane, values[:, :-1]], axis=1)
    return [values - shifted, values - jnp.roll(values, 1, 2), values - jnp.roll(values, 1, 3)]


def velocity_stack(values, velocity):
    positive = jnp.maximum(velocity, 0.0)
    negative = jnp.minimum(velocity, 0.0)
    rank_count = values.shape[0]
    forward = (values[None] * positive[:, None]).reshape(3 * rank_count, -1)
    backward = (values[None] * negative[:, None]).reshape(3 * rank_count, -1)
    return jnp.concatenate([forward, backward], axis=0)


def mixing(space_terms):
    rank_count = space_terms.shape[0]
    backward = [
        space_terms[:, dimension * rank_count : (dimension + 1) * rank_count]
        for dimension in range(3)
    ]
    forward = [-section.T for section in backward]
    return jnp.concatenate(
        backward + forward + [space_terms[:, 3 * rank_count : 4 * rank_count]], axis=1
    )


def kinetic_update(padded, rates, flux_blocks, weights, moments):
    center = padded[:, 1:-1]
    backward = [
        center - padded[:, :-2],
        center - jnp.roll(center, 1, 2),
        center - jnp.roll(center, 1, 3),
    ]
    forward = [
        padded[:, 2:] - center,
        jnp.roll(center, -1, 2) - center,
        jnp.roll(center, -1, 3) - center,
    ]
    stacked = jnp.concatenate(backward + forward, axis=0).reshape(6 * center.shape[0], -1)
    flat_center = flatten_rows(center)
    transport = jnp.dot(flux_blocks, stacked, precision=highest)
    density = jnp.dot(weights, flat_center, precision=highest)
    change = -transport + rates.reshape(1, -1) * (moments[:, None] * density[None, :] - flat_center)
    return (flat_center + time_step * change).reshape(center.shape)


def velocity_update(values, mixing_blocks, velocity, profile, column_means):
    rank_count = values.shape[0]
    stacked = jnp.concatenate([velocity_stack(values, velocity), values], axis=0)
    change = -jnp.dot(mixing_blocks, stacked, precision=highest)
    source = jnp.dot(mixing_blocks[:, 6 * rank_count :], column_means, precision=highest)
    return values + time_step * (change + source[:, None] * profile[None, :])


def core_update(current, space_terms, point_terms, weights, moments):
    rank_count = current.shape[0]
    scaled = jnp.dot(space_terms[:, 3 * rank_count : 4 * rank_count], current, precision=highest)
    change = -scaled + jnp.outer(jnp.dot(scaled, weights, precision=highest), moments)
    for dimension in range(3):
        section = space_terms[:, dimension * rank_count : (dimension + 1) * rank_count]
        plus_block = point_terms[:, dimension * rank_count : (dimension + 1) * rank_count]
        minus_block = point_terms[:, (dimension + 3) * rank_count : (dimension + 4) * rank_count]
        change = change - jnp.dot(
            jnp.dot(section, current, precision=highest), plus_block.T, precision=highest
        )
        change = change + jnp.dot(
            jnp.dot(section.T, current, precision=highest), minus_block.T, precision=highest
        )
    return current + time_step * change


def cell_share(values):
    merged = values.reshape(values.shape[0], values.shape[1] * values.shape[2], values.shape[3])
    return flatten_rows(merged)


def combine(space_part, point_part):
    space_total = lax.psum(space_part, "space")
    point_total = lax.psum(point_part, "vel")
    return (space_total, point_total)


def project(
    space_state,
    lower_plane,
    space_old,
    rates,
    point_state,
    point_old,
    velocity,
    profile,
    cells_total,
    points_total,
):
    rank_count = space_state.shape[0]
    share_profile = profile[None]
    ones_row = jnp.ones_like(share_profile)
    space_part = products(cell_share(space_state), cell_share(space_state), cells_total)
    point_part = products(
        point_state, jnp.concatenate([point_state, ones_row, share_profile], axis=0), points_total
    )
    space_sums, point_sums = combine(space_part, point_part)
    space_inverse = triangular_inverse(space_sums)
    point_inverse = triangular_inverse(point_sums[:, :rank_count])
    weights = jnp.dot(point_inverse, point_sums[:, rank_count], precision=highest)
    moments = jnp.dot(point_inverse, point_sums[:, rank_count + 1], precision=highest)
    space_new = apply_rows(space_inverse, space_state)
    point_new = jnp.dot(point_inverse, point_state, precision=highest)
    new_lower = apply_rows(space_inverse, lower_plane)
    space_items = lower_differences(space_new, new_lower) + [rates[None] * space_new, space_old]
    space_others = jnp.concatenate([cell_share(member) for member in space_items], axis=0)
    space_part = products(cell_share(space_new), space_others, cells_total)
    point_others = jnp.concatenate([velocity_stack(point_new, velocity), point_old], axis=0)
    point_part = products(point_new, point_others, points_total)
    space_terms, point_terms = combine(space_part, point_part)
    return (space_new, point_new, space_terms, point_terms, weights, moments)


def per_device(space_factor, core_matrix, velocity_factor, collision_rates):
    rank_count = core_matrix.shape[0]
    point_rows = velocity_factor.shape[1]
    cells_total = (
        space_factor.shape[1]
        * space_factor.shape[2]
        * space_factor.shape[3]
        * lax.axis_size("space")
    )
    points_total = point_rows * lax.axis_size("vel")
    velocity, profile = velocity_grid(lax.axis_index("vel") * point_rows, point_rows)
    start_lower = from_behind(space_factor[:, -1:], "space", 1)
    basis_space, basis_point, space_terms, point_terms, weights, moments = project(
        space_factor,
        start_lower,
        space_factor,
        collision_rates,
        velocity_factor,
        velocity_factor,
        velocity,
        profile,
        cells_total,
        points_total,
    )
    current = jnp.dot(
        jnp.dot(space_terms[:, 4 * rank_count :], core_matrix, precision=highest),
        point_terms[:, 6 * rank_count :].T,
        precision=highest,
    )
    flux_blocks = point_terms[:, : 6 * rank_count]
    kinetic = apply_rows(current.T, basis_space)
    for substep in range(SUB):
        padded = padded_2(kinetic, (("space", 1),), 1)
        kinetic = kinetic_update(padded, collision_rates, flux_blocks, weights, moments)
    lower_plane = from_behind(kinetic[:, -1:], "space", 1)
    mixing_blocks = mixing(space_terms)
    spread_point = jnp.dot(current, basis_point, precision=highest)
    for substep in range(SUB):
        local_total = jnp.sum(spread_point, axis=1) / points_total
        column_means = lax.psum(local_total, "vel")
        spread_point = velocity_update(spread_point, mixing_blocks, velocity, profile, column_means)
    fresh_space, fresh_point, space_terms, point_terms, weights, moments = project(
        kinetic,
        lower_plane,
        basis_space,
        collision_rates,
        spread_point,
        basis_point,
        velocity,
        profile,
        cells_total,
        points_total,
    )
    current = jnp.dot(
        jnp.dot(space_terms[:, 4 * rank_count :], current, precision=highest),
        point_terms[:, 6 * rank_count :].T,
        precision=highest,
    )
    for substep in range(SUB):
        current = core_update(current, space_terms, point_terms, weights, moments)
    return (fresh_space, current, fresh_point)


def solution(mesh):
    return jax.shard_map(
        per_device,
        mesh=mesh,
        in_specs=(P(None, "space", None, None), P(), P(None, "vel"), P("space", None, None)),
        out_specs=(P(None, "space", None, None), P(), P(None, "vel")),
        check_vma=False,
    )
```

profile of v0, /device:TPU:96, one launch (start us, length us, event | category | flops | bytes accessed | tf_op | source)
XLA Modules:
  0.0 670.9 jit_solution(7387218225295782337)
XLA Ops:
  7.5 73.3 %psum.77 = f32[32,32]{0,1:T(8,128)S(1)} all-reduce(f32[32,32]{0,1:T(8,128)S(1)} %fusion.63), channel_id=1, replica_groups=mesh['space'=16,'vel'=8] {'space'}, use_global_device_ids=true, to_apply=%region_0.1 | all-reduce | flops 1024 | bytes 8192 | tf_op jit(solution)/shard_map/psum | solution.py:153
  101.9 19.6 %psum.79 = f32[32,34]{0,1:T(8,128)S(1)} all-reduce(f32[32,34]{0,1:T(8,128)S(1)} %fusion.59), channel_id=1, replica_groups=mesh['space'=16,'vel'=8] {'vel'}, use_global_device_ids=true, to_apply=%region_5.8 | all-reduce | flops 1088 | bytes 8704 | tf_op jit(solution)/shard_map/psum | solution.py:154
  135.9 11.1 %fusion.54 = f32[32,224]{1,0:T(8,128)S(1)} fusion(f32[32,13824]{1,0:T(8,128)S(1)} %fusion.292, f32[32,13824]{1,0:T(8,128)S(1)} %copy-done.16, f32[96,13824]{1,0:T(8,128)S(1)} %bitcast.366, f32[96,13824]{1,0:T(8,128)S(1)} %bitcast.365), kind=kOutput, calls=%fused_computation.74 | convolution fusion | flops 1195285504 | bytes 14184448 | tf_op jit(solution)/shard_map/dot_general | solution.py:57
  149.3 23.7 %psum.80 = f32[32,224]{1,0:T(8,128)S(1)} all-reduce(f32[32,224]{1,0:T(8,128)S(1)} %fusion.54), channel_id=1, replica_groups=mesh['space'=16,'vel'=8] {'vel'}, use_global_device_ids=true, to_apply=%region_6.9 | all-reduce | flops 7168 | bytes 57344 | tf_op jit(solution)/shard_map/psum | solution.py:154
  185.6 69.8 %psum.78 = f32[32,160]{1,0:T(8,128)S(1)} all-reduce(f32[32,160]{1,0:T(8,128)S(1)} %convolution_multiply_fusion.1), channel_id=1, replica_groups=mesh['space'=16,'vel'=8] {'space'}, use_global_device_ids=true, to_apply=%region_3.6 | all-reduce | flops 5120 | bytes 40960 | tf_op jit(solution)/shard_map/psum | solution.py:153
  267.3 13.0 %psum.83 = f32[32]{0:T(128)S(1)} all-reduce(f32[32]{0:T(128)S(1)} %broadcast_multiply_fusion.12), channel_id=1, replica_groups=mesh['space'=16,'vel'=8] {'vel'}, use_global_device_ids=true, to_apply=%region_10.13 | all-reduce | flops 32 | bytes 256 | tf_op jit(solution)/shard_map/psum | solution.py:233
  280.5 6.7 %broadcast_multiply_fusion.7 = (f32[3,32,13824]{2,1,0:T(8,128)}, f32[3,32,13824]{2,1,0:T(8,128)}) fusion(f32[32,13824]{1,0:T(8,128)} %get-tuple-element.52, f32[3,13824]{1,0:T(4,128)S(1)} %get-tuple-element.45, f32[3,13824]{1,0:T(4,128)} %copy-done.7), kind=kLoop, calls=%fused_computation.60 | loop fusion | flops 2654208 | bytes 12718080 | tf_op jit(solution)/shard_map/mul | solution.py:85
  288.0 10.7 %fusion.290 = (f32[32]{0:T(128)S(1)}, f32[32,13824]{1,0:T(8,128)S(1)}) fusion(f32[32,13824]{1,0:T(8,128)} %get-tuple-element.52, f32[13824]{0:T(1024)} %fusion.118, f32[32]{0:T(128)S(1)} %convolution_bitcast_fusion.10, f32[32,224]{1,0:T(8,128)} %concatenate.176, f32[96,13824]{1,0:T(8,128)} %bitcast.358, f32[96,13824]{1,0:T(8,128)} %bitcast.357), kind=kOutput, calls=%fused_computation.412 | convolution fusion | flops 1197490176 | bytes 14240000 | tf_op jit(solution)/shard_map/dot_general | solution.py:125
  303.9 12.4 %psum.84 = f32[32]{0:T(128)S(1)} all-reduce(f32[32]{0:T(128)S(1)} %broadcast_multiply_fusion.11), channel_id=1, replica_groups=mesh['space'=16,'vel'=8] {'vel'}, use_global_device_ids=true, to_apply=%region_12.15 | all-reduce | flops 32 | bytes 256 | tf_op jit(solution)/shard_map/psum | solution.py:233
  316.5 11.5 %fusion.291 = (f32[32]{0:T(128)S(1)}, f32[32,13824]{1,0:T(8,128)}) fusion(f32[32,13824]{1,0:T(8,128)} %copy-done.19, f32[13824]{0:T(1024)S(1)} %copy-done.30, f32[32]{0:T(128)S(1)} %convolution_bitcast_fusion.9, f32[32,224]{1,0:T(8,128)} %concatenate.176, f32[96,13824]{1,0:T(8,128)} %bitcast.360, f32[96,13824]{1,0:T(8,128)} %bitcast.359), kind=kOutput, calls=%fused_computation.413 | convolution fusion | flops 1197490176 | bytes 14240000 | tf_op jit(solution)/shard_map/dot_general | solution.py:125
  328.0 12.8 %psum.85 = f32[32]{0:T(128)S(1)} all-reduce(f32[32]{0:T(128)S(1)} %broadcast_multiply_fusion.10), channel_id=1, replica_groups=mesh['space'=16,'vel'=8] {'vel'}, use_global_device_ids=true, to_apply=%region_14.17 | all-reduce | flops 32 | bytes 256 | tf_op jit(solution)/shard_map/psum | solution.py:233
  343.9 7.3 %fusion.1 = f32[32,13824]{1,0:T(8,128)S(1)} fusion(f32[32,13824]{1,0:T(8,128)S(1)} %copy-done.18, f32[32,224]{1,0:T(8,128)S(1)} %copy-done.33, f32[96,13824]{1,0:T(8,128)S(1)} %bitcast.364, f32[96,13824]{1,0:T(8,128)S(1)} %bitcast.363, f32[32]{0:T(128)S(1)} %convolution_bitcast_fusion.8, f32[13824]{0:T(1024)S(1)} %copy-done.30), kind=kOutput, calls=%fused_computation.2 | convolution fusion | flops 1197047808 | bytes 14239872 | tf_op jit(solution)/shard_map/dot_general | solution.py:125
  354.4 23.2 %psum.86 = f32[32,34]{0,1:T(8,128)S(1)} all-reduce(f32[32,34]{0,1:T(8,128)S(1)} %fusion.57), channel_id=1, replica_groups=mesh['space'=16,'vel'=8] {'vel'}, use_global_device_ids=true, to_apply=%region_15.18 | all-reduce | flops 1088 | bytes 8704 | tf_op jit(solution)/shard_map/psum | solution.py:154
  390.6 10.9 %fusion.51 = f32[32,224]{1,0:T(8,128)S(1)} fusion(f32[32,13824]{1,0:T(8,128)S(1)} %fusion.298, f32[32,13824]{1,0:T(8,128)S(1)} %copy-done.5, f32[96,13824]{1,0:T(8,128)S(1)} %bitcast.362, f32[96,13824]{1,0:T(8,128)S(1)} %bitcast.361), kind=kOutput, calls=%fused_computation.73 | convolution fusion | flops 1195285504 | bytes 14184448 | tf_op jit(solution)/shard_map/dot_general | solution.py:57
  401.6 23.6 %psum.87 = f32[32,224]{1,0:T(8,128)S(1)} all-reduce(f32[32,224]{1,0:T(8,128)S(1)} %fusion.51), channel_id=1, replica_groups=mesh['space'=16,'vel'=8] {'vel'}, use_global_device_ids=true, to_apply=%region_16.19 | all-reduce | flops 7168 | bytes 57344 | tf_op jit(solution)/shard_map/psum | solution.py:154
  425.2 5.6 collective-permute-start.2
  438.4 7.3 %fusion.38 = f32[32,8192]{1,0:T(8,128)S(1)} fusion(f32[32,8192]{1,0:T(8,128)S(1)} %fusion.293, f32[24,8,64,128]{3,2,1,0:T(8,128)S(1)} %bitcast.354, f32[8192]{0:T(1024)S(1)} %bitcast.381, f32[32]{0:T(128)S(1)} %copy-done.34, f32[8192]{0:T(1024)S(1)} %bitcast.375, f32[32,224]{1,0:T(8,128)S(1)} %psum.80), kind=kOutput, calls=%fused_computation.44 | convolution fusion | flops 605552640 | bytes 8482944 | tf_op jit(solution)/shard_map/dot_general | solution.py:116
  447.2 6.2 collective-permute-start.4
  460.8 7.3 %fusion.36 = f32[32,8192]{1,0:T(8,128)S(1)} fusion(f32[32,8192]{1,0:T(8,128)S(1)} %fusion.38, f32[24,8,64,128]{3,2,1,0:T(8,128)S(1)} %bitcast.355, f32[8192]{0:T(1024)S(1)} %bitcast.382, f32[32]{0:T(128)S(1)} %copy-done.34, f32[8192]{0:T(1024)S(1)} %bitcast.376, f32[32,224]{1,0:T(8,128)S(1)} %psum.80), kind=kOutput, calls=%fused_computation.41 | convolution fusion | flops 605552640 | bytes 8482944 | tf_op jit(solution)/shard_map/dot_general | solution.py:116
  469.6 5.6 collective-permute-start.6
  482.0 7.2 %fusion.34 = f32[32,8192]{1,0:T(8,128)S(1)} fusion(f32[32,8192]{1,0:T(8,128)S(1)} %fusion.36, f32[24,8,64,128]{3,2,1,0:T(8,128)S(1)} %bitcast.356, f32[8192]{0:T(1024)S(1)} %bitcast.380, f32[32]{0:T(128)S(1)} %copy-done.34, f32[8192]{0:T(1024)S(1)} %bitcast.377, f32[32,224]{1,0:T(8,128)S(1)} %psum.80), kind=kOutput, calls=%fused_computation.38 | convolution fusion | flops 605552640 | bytes 8482944 | tf_op jit(solution)/shard_map/dot_general | solution.py:116
  490.3 74.4 %psum.81 = f32[32,32]{0,1:T(8,128)S(1)} all-reduce(f32[32,32]{0,1:T(8,128)S(1)} %convolution_multiply_fusion.2), channel_id=1, replica_groups=mesh['space'=16,'vel'=8] {'space'}, use_global_device_ids=true, to_apply=%region_7.10 | all-reduce | flops 1024 | bytes 8192 | tf_op jit(solution)/shard_map/psum | solution.py:153
  574.2 9.2 %collective-permute-done.7 = f32[32,1,16,128]{3,2,1,0:T(8,128)S(1)} collective-permute-done((f32[32,1,16,128]{3,2,1,0:T(8,128)S(1)}, f32[32,1,16,128]{3,2,1,0:T(8,128)S(1)}, u32[]{:S(2)}, u32[]{:S(2)}) %collective-permute-start.7) | collective-permute-done | bytes 262176 | tf_op jit(solution)/shard_map/ppermute | solution.py:17
  591.3 69.5 %psum.82 = f32[32,160]{1,0:T(8,128)S(1)} all-reduce(f32[32,160]{1,0:T(8,128)S(1)} %convolution_multiply_fusion), channel_id=1, replica_groups=mesh['space'=16,'vel'=8] {'space'}, use_global_device_ids=true, to_apply=%region_8.11 | all-reduce | flops 5120 | bytes 40960 | tf_op jit(solution)/shard_map/psum | solution.py:153
  (278 shorter events, 144.7 us)
Async XLA Ops:
  0.6 255.4 %copy-start = (f32[32,32]{1,0:T(8,128)S(1)}, f32[32,32]{1,0:T(8,128)}, u32[]{:S(2)}) copy-start(f32[32,32]{1,0:T(8,128)} %param.8) | copy-start | bytes 12292
  2.3 171.5 %collective-permute-start = (f32[32,1,16,128]{3,2,1,0:T(8,128)}, f32[32,1,16,128]{3,2,1,0:T(8,128)}, u32[]{:S(2)}, u32[]{:S(2)}) collective-permute-start(f32[32,1,16,128]{3,2,1,0:T(8,128)} %slice.264), channel_id=1, source_target_pairs={{120,0},{0,8},{8,16},{16,24},{24,32},{32,40},{40,48},{48,56},{56,6... | collective-permute-start | bytes 786440 | tf_op jit(solution)/shard_map/ppermute | solution.py:17
  97.8 36.3 %copy-start.36 = (f32[34]{0:T(128)}, f32[34]{0:T(128)S(1)}, u32[]{:S(2)}) copy-start(f32[34]{0:T(128)S(1)} %pad.64.clone) | copy-start | bytes 412
  121.6 12.6 %copy-start.25 = (f32[32,34]{0,1:T(8,128)}, f32[32,34]{0,1:T(8,128)S(1)}, u32[]{:S(2)}) copy-start(f32[32,34]{0,1:T(8,128)S(1)} %psum.79) | copy-start | bytes 13060
  135.9 38.0 %copy-start.27 = (f32[32,32]{1,0:T(8,128)S(1)}, f32[32,32]{1,0:T(8,128)}, u32[]{:S(2)}) copy-start(f32[32,32]{1,0:T(8,128)} %copy-done.26) | copy-start | bytes 12292
  179.9 76.5 %copy-start.4 = (f32[32,13824]{1,0:T(8,128)S(1)}, f32[32,13824]{1,0:T(8,128)}, u32[]{:S(2)}) copy-start(f32[32,13824]{1,0:T(8,128)} %copy-done.3) | copy-start | bytes 5308420
  255.4 24.9 %copy-start.20 = (f32[32,160]{1,0:T(8,128)}, f32[32,160]{1,0:T(8,128)S(1)}, u32[]{:S(2)}) copy-start(f32[32,160]{1,0:T(8,128)S(1)} %psum.78) | copy-start | bytes 61444
  287.9 10.7 %copy-start.8 = (f32[3,13824]{1,0:T(4,128)S(1)}, f32[3,13824]{1,0:T(4,128)}, u32[]{:S(2)}) copy-start(f32[3,13824]{1,0:T(4,128)} %copy-done.7) | copy-start | bytes 497668
  298.6 17.6 %copy-start.21 = (f32[32,160]{1,0:T(8,128)S(1)}, f32[32,160]{1,0:T(8,128)}, u32[]{:S(2)}) copy-start(f32[32,160]{1,0:T(8,128)} %copy-done.20) | copy-start | bytes 61444
  298.7 17.8 %copy-start.30 = (f32[13824]{0:T(1024)S(1)}, f32[13824]{0:T(1024)}, u32[]{:S(2)}) copy-start(f32[13824]{0:T(1024)} %fusion.118) | copy-start | bytes 165892
  343.8 8.6 %copy-start.32 = (f32[1,13824]{1,0:T(1,128)S(1)}, f32[1,13824]{1,0:T(1,128)}, u32[]{:S(2)}) copy-start(f32[1,13824]{1,0:T(1,128)} %copy-done.31) | copy-start | bytes 165892
  343.8 8.6 %copy-start.37 = (f32[34]{0:T(128)S(1)}, f32[34]{0:T(128)}, u32[]{:S(2)}) copy-start(f32[34]{0:T(128)} %copy-done.36) | copy-start | bytes 412
  390.5 40.9 %collective-permute-start.1 = (f32[32,1,16,128]{3,2,1,0:T(8,128)}, f32[32,1,16,128]{3,2,1,0:T(8,128)}, u32[]{:S(2)}, u32[]{:S(2)}) collective-permute-start(f32[32,1,16,128]{3,2,1,0:T(8,128)} %get-tuple-element.44), channel_id=1, source_target_pairs={{0,8},{8,16},{16,24},{24,32},{32,40},{40,48},{48,56},{56,64},{64,7... | collective-permute-start | bytes 786440 | tf_op jit(solution)/shard_map/ppermute | solution.py:27
  390.6 40.2 %copy-start.35 = (f32[32,1]{0,1:T(1,128)S(1)}, f32[32,1]{0,1:T(1,128)}, u32[]{:S(2)}) copy-start(f32[32,1]{0,1:T(1,128)} %convolution_bitcast_fusion.11) | copy-start | bytes 388
  390.6 41.9 %copy-start.24 = (f32[32,4,1,128]{3,2,1,0:T(1,128)S(1)}, f32[32,4,1,128]{3,2,1,0:T(1,128)}, u32[]{:S(2)}) copy-start(f32[32,4,1,128]{3,2,1,0:T(1,128)} %get-tuple-element.42) | copy-start | bytes 196612
  425.2 8.9 %copy-start.14 = (f32[32,4,16,127]{3,2,1,0:T(8,128)S(1)}, f32[32,4,16,127]{3,2,1,0:T(8,128)}, u32[]{:S(2)}) copy-start(f32[32,4,16,127]{3,2,1,0:T(8,128)} %get-tuple-element.36) | copy-start | bytes 3121156
  425.2 8.9 %copy-start.15 = (f32[32,4,16,1]{3,2,1,0:T(8,128)S(1)}, f32[32,4,16,1]{3,2,1,0:T(8,128)}, u32[]{:S(2)}) copy-start(f32[32,4,16,1]{3,2,1,0:T(8,128)} %get-tuple-element.38) | copy-start | bytes 24580
  425.2 12.4 %collective-permute-start.2 = (f32[32,1,16,128]{3,2,1,0:T(8,128)}, f32[32,1,16,128]{3,2,1,0:T(8,128)S(1)}, u32[]{:S(2)}, u32[]{:S(2)}) collective-permute-start(f32[32,1,16,128]{3,2,1,0:T(8,128)} %get-tuple-element.43), channel_id=1, source_target_pairs={{8,0},{16,8},{24,16},{32,24},{40,32},{48,40},{56,48},{64,56},{72,6... | collective-permute-start | bytes 786440 | tf_op jit(solution)/shard_map/ppermute | solution.py:29
  447.0 12.3 %collective-permute-start.3 = (f32[32,1,16,128]{3,2,1,0:T(8,128)S(1)}, f32[32,1,16,128]{3,2,1,0:T(8,128)S(1)}, u32[]{:S(2)}, u32[]{:S(2)}) collective-permute-start(f32[32,1,16,128]{3,2,1,0:T(8,128)S(1)} %get-tuple-element.34), channel_id=1, source_target_pairs={{0,8},{8,16},{16,24},{24,32},{32,40},{40,48},{48,56},{56,64},{64,7... | collective-permute-start | bytes 786440 | tf_op jit(solution)/shard_map/ppermute | solution.py:27
  447.2 12.9 %collective-permute-start.4 = (f32[32,1,16,128]{3,2,1,0:T(8,128)S(1)}, f32[32,1,16,128]{3,2,1,0:T(8,128)S(1)}, u32[]{:S(2)}, u32[]{:S(2)}) collective-permute-start(f32[32,1,16,128]{3,2,1,0:T(8,128)S(1)} %get-tuple-element.33), channel_id=1, source_target_pairs={{8,0},{16,8},{24,16},{32,24},{40,32},{48,40},{56,48},{64,56},{72,6... | collective-permute-start | bytes 786440 | tf_op jit(solution)/shard_map/ppermute | solution.py:29
  469.4 11.1 %collective-permute-start.5 = (f32[32,1,16,128]{3,2,1,0:T(8,128)S(1)}, f32[32,1,16,128]{3,2,1,0:T(8,128)S(1)}, u32[]{:S(2)}, u32[]{:S(2)}) collective-permute-start(f32[32,1,16,128]{3,2,1,0:T(8,128)S(1)} %get-tuple-element.24), channel_id=1, source_target_pairs={{0,8},{8,16},{16,24},{24,32},{32,40},{40,48},{48,56},{56,64},{64,7... | collective-permute-start | bytes 786440 | tf_op jit(solution)/shard_map/ppermute | solution.py:27
  469.6 11.7 %collective-permute-start.6 = (f32[32,1,16,128]{3,2,1,0:T(8,128)S(1)}, f32[32,1,16,128]{3,2,1,0:T(8,128)S(1)}, u32[]{:S(2)}, u32[]{:S(2)}) collective-permute-start(f32[32,1,16,128]{3,2,1,0:T(8,128)S(1)} %get-tuple-element.23), channel_id=1, source_target_pairs={{8,0},{16,8},{24,16},{32,24},{40,32},{48,40},{56,48},{64,56},{72,6... | collective-permute-start | bytes 786440 | tf_op jit(solution)/shard_map/ppermute | solution.py:29
  573.6 9.8 %collective-permute-start.7 = (f32[32,1,16,128]{3,2,1,0:T(8,128)S(1)}, f32[32,1,16,128]{3,2,1,0:T(8,128)S(1)}, u32[]{:S(2)}, u32[]{:S(2)}) collective-permute-start(f32[32,1,16,128]{3,2,1,0:T(8,128)S(1)} %slice.379), channel_id=1, source_target_pairs={{120,0},{0,8},{8,16},{16,24},{24,32},{32,40},{40,48},{48,56},{56,6... | collective-permute-start | bytes 786440 | tf_op jit(solution)/shard_map/ppermute | solution.py:17
  586.2 84.5 %copy-start.1 = (f32[32,32]{1,0:T(8,128)S(1)}, f32[32,32]{1,0:T(8,128)}, u32[]{:S(2)}) copy-start(f32[32,32]{1,0:T(8,128)} %param.8) | copy-start | bytes 12292
  (23 other events, 82.0 us)
where the time goes:
time: 679 us; the launch traced here: 671 us
  blocking collectives  415 us (61%)
  matrix products  126 us (19%)
  other arithmetic  65.2 us (10%)
  waiting for transfers between devices  22.5 us (3%)
  starting transfers between devices  19.1 us (3%)
  local copies, waits for them, and re-layouts  19 us (3%)
    psum x4, blocking collectives, combine(): space_total = lax.psum(space_part, 'space')  287 us
    psum x4, blocking collectives, combine(): point_total = lax.psum(point_part, 'vel')  90.2 us
    dot_general x8, matrix products, products(): lax.dot_general(leading, others, (((1,), (1,)), ((), ())), precision=high...  42.7 us
    psum x3, blocking collectives, per_device(): column_means = lax.psum(local_total, 'vel')  38.2 us
    dot_general x3, matrix products, velocity_update(): change = -jnp.dot(mixing_blocks, stacked, precision=highest)  29.5 us
    dot_general x3, matrix products, kinetic_update(): transport = jnp.dot(flux_blocks, stacked, precision=highest)  21.8 us
    mul x5, other arithmetic, velocity_stack(): forward = (values[None] * positive[:, None]).reshape(3 * rank_count, -1)  18.3 us
    ppermute x3, starting transfers between devices, padded_2(): lax.ppermute(head, axis, [((i + 1) % count, i) for i in range(count)])  17.3 us
  transfers between devices with their start and end apart: 8, of which 4 were waited for; matrix products, arithmetic and copies ran while one was open for 10% of the time, Pallas kernels for 0%

commit v1 on v0

--- a/solution.py
+++ b/solution.py
@@ -151,7 +151,7 @@
 
 def combine(space_part, point_part):
     space_total = lax.psum(space_part, "space")
-    point_total = lax.psum(point_part, "vel")
+    point_total = jnp.sum(lax.all_gather(point_part, "vel"), axis=0)
     return (space_total, point_total)
 
 

time: 679 us -> 640 us (0.943)
  blocking collectives: 415 us -> 376 us
    psum x4 -> x0, blocking collectives: 90.2 us -> none  [combine(): point_total = lax.psum(point_part, 'vel')]
    all_gather x0 -> x4, blocking collectives: none -> 55 us  [combine(): point_total = jnp.sum(lax.all_gather(point_part, 'vel'), axis=0)]
  transfers between devices with their start and end apart: 8 -> 8, of which waited for: 4 -> 4; matrix products, arithmetic and copies ran while one was open for 10% -> 11% of each run, Pallas kernels for 0% -> 0%
where the time goes in v1:
time: 640 us; the launch traced here: 628 us
  blocking collectives  376 us (59%)
  matrix products  125 us (20%)
  other arithmetic  65.7 us (10%)
  waiting for transfers between devices  20.8 us (3%)
  starting transfers between devices  18.9 us (3%)
  local copies, waits for them, and re-layouts  17.5 us (3%)
    psum x4, blocking collectives, combine(): space_total = lax.psum(space_part, 'space')  287 us
    all_gather x4, blocking collectives, combine(): point_total = jnp.sum(lax.all_gather(point_part, 'vel'), axis=0)  55 us
    dot_general x8, matrix products, products(): lax.dot_general(leading, others, (((1,), (1,)), ((), ())), precision=high...  42.7 us
    psum x3, blocking collectives, per_device(): column_means = lax.psum(local_total, 'vel')  34.1 us
    dot_general x3, matrix products, velocity_update(): change = -jnp.dot(mixing_blocks, stacked, precision=highest)  29.6 us
    dot_general x3, matrix products, kinetic_update(): transport = jnp.dot(flux_blocks, stacked, precision=highest)  21.8 us
    mul x5, other arithmetic, velocity_stack(): forward = (values[None] * positive[:, None]).reshape(3 * rank_count, -1)  18.3 us
    ppermute x3, starting transfers between devices, padded_2(): lax.ppermute(head, axis, [((i + 1) % count, i) for i in range(count)])  17.1 us
  transfers between devices with their start and end apart: 8, of which 4 were waited for; matrix products, arithmetic and copies ran while one was open for 11% of the time, Pallas kernels for 0%

profile of v1, /device:TPU:96, one launch (start us, length us, event | category | flops | bytes accessed | tf_op | source)
XLA Modules:
  0.0 628.1 jit_solution(18153081705300863856)
XLA Ops:
  7.5 73.3 %psum.49 = f32[32,32]{0,1:T(8,128)S(1)} all-reduce(f32[32,32]{0,1:T(8,128)S(1)} %fusion.63), channel_id=1, replica_groups=mesh['space'=16,'vel'=8] {'space'}, use_global_device_ids=true, to_apply=%region_0.1 | all-reduce | flops 1024 | bytes 8192 | tf_op jit(solution)/shard_map/psum | solution.py:153
  101.0 13.2 %all-gather = f32[256,34]{1,0:T(8,128)S(1)} all-gather(f32[32,34]{1,0:T(8,128)S(1)} %fusion.59), channel_id=2, replica_groups=mesh['space'=16,'vel'=8] {'vel'}, dimensions={0}, use_global_device_ids=true | all-gather | bytes 39168 | tf_op jit(solution)/shard_map/all_gather | solution.py:154
  130.2 11.1 %fusion.54 = f32[32,224]{1,0:T(8,128)S(1)} fusion(f32[32,13824]{1,0:T(8,128)S(1)} %fusion.292, f32[32,13824]{1,0:T(8,128)S(1)} %copy-done.17, f32[96,13824]{1,0:T(8,128)S(1)} %bitcast.380, f32[96,13824]{1,0:T(8,128)S(1)} %bitcast.379), kind=kOutput, calls=%fused_computation.74 | convolution fusion | flops 1195285504 | bytes 14184448 | tf_op jit(solution)/shard_map/dot_general | solution.py:57
  141.3 13.9 %all-gather.1 = f32[256,224]{1,0:T(8,128)} all-gather(f32[32,224]{1,0:T(8,128)S(1)} %fusion.54), channel_id=3, replica_groups=mesh['space'=16,'vel'=8] {'vel'}, dimensions={0}, use_global_device_ids=true | all-gather | bytes 258048 | tf_op jit(solution)/shard_map/all_gather | solution.py:154
  166.6 69.8 %psum.50 = f32[32,160]{1,0:T(8,128)S(1)} all-reduce(f32[32,160]{1,0:T(8,128)S(1)} %convolution_multiply_fusion.1), channel_id=1, replica_groups=mesh['space'=16,'vel'=8] {'space'}, use_global_device_ids=true, to_apply=%region_3.6 | all-reduce | flops 5120 | bytes 40960 | tf_op jit(solution)/shard_map/psum | solution.py:153
  248.3 10.2 %psum.53 = f32[32]{0:T(128)S(1)} all-reduce(f32[32]{0:T(128)S(1)} %broadcast_multiply_fusion.12), channel_id=1, replica_groups=mesh['space'=16,'vel'=8] {'vel'}, use_global_device_ids=true, to_apply=%region_10.13 | all-reduce | flops 32 | bytes 256 | tf_op jit(solution)/shard_map/psum | solution.py:233
  258.7 6.7 %broadcast_multiply_fusion.7 = (f32[3,32,13824]{2,1,0:T(8,128)}, f32[3,32,13824]{2,1,0:T(8,128)}) fusion(f32[32,13824]{1,0:T(8,128)} %get-tuple-element.56, f32[3,13824]{1,0:T(4,128)S(1)} %get-tuple-element.49, f32[3,13824]{1,0:T(4,128)} %copy-done.7), kind=kLoop, calls=%fused_computation.60 | loop fusion | flops 2654208 | bytes 12718080 | tf_op jit(solution)/shard_map/mul | solution.py:85
  266.2 10.7 %fusion.290 = (f32[32]{0:T(128)S(1)}, f32[32,13824]{1,0:T(8,128)S(1)}) fusion(f32[32,13824]{1,0:T(8,128)} %get-tuple-element.56, f32[13824]{0:T(1024)} %fusion.118, f32[32]{0:T(128)S(1)} %convolution_bitcast_fusion.10, f32[32,224]{1,0:T(8,128)} %concatenate.176, f32[96,13824]{1,0:T(8,128)} %bitcast.374, f32[96,13824]{1,0:T(8,128)} %bitcast.373), kind=kOutput, calls=%fused_computation.416 | convolution fusion | flops 1197490176 | bytes 14240000 | tf_op jit(solution)/shard_map/dot_general | solution.py:125
  282.1 11.5 %psum.54 = f32[32]{0:T(128)S(1)} all-reduce(f32[32]{0:T(128)S(1)} %broadcast_multiply_fusion.11), channel_id=1, replica_groups=mesh['space'=16,'vel'=8] {'vel'}, use_global_device_ids=true, to_apply=%region_12.15 | all-reduce | flops 32 | bytes 256 | tf_op jit(solution)/shard_map/psum | solution.py:233
  293.8 11.6 %fusion.291 = (f32[32]{0:T(128)S(1)}, f32[32,13824]{1,0:T(8,128)}) fusion(f32[32,13824]{1,0:T(8,128)} %copy-done.20, f32[13824]{0:T(1024)} %fusion.118, f32[32]{0:T(128)S(1)} %convolution_bitcast_fusion.9, f32[32,224]{1,0:T(8,128)S(1)} %copy-done.32, f32[96,13824]{1,0:T(8,128)} %bitcast.376, f32[96,13824]{1,0:T(8,128)} %bitcast.375), kind=kOutput, calls=%fused_computation.417 | convolution fusion | flops 1197490176 | bytes 14240000 | tf_op jit(solution)/shard_map/dot_general | solution.py:125
  305.3 12.4 %psum.55 = f32[32]{0:T(128)S(1)} all-reduce(f32[32]{0:T(128)S(1)} %broadcast_multiply_fusion.10), channel_id=1, replica_groups=mesh['space'=16,'vel'=8] {'vel'}, use_global_device_ids=true, to_apply=%region_14.17 | all-reduce | flops 32 | bytes 256 | tf_op jit(solution)/shard_map/psum | solution.py:233
  320.8 7.3 %fusion.1 = f32[32,13824]{1,0:T(8,128)S(1)} fusion(f32[32,13824]{1,0:T(8,128)S(1)} %copy-done.19, f32[32,224]{1,0:T(8,128)S(1)} %copy-done.33, f32[96,13824]{1,0:T(8,128)S(1)} %bitcast.378, f32[96,13824]{1,0:T(8,128)S(1)} %bitcast.377, f32[32]{0:T(128)S(1)} %convolution_bitcast_fusion.8, f32[13824]{0:T(1024)S(1)} %copy-done.29), kind=kOutput, calls=%fused_computation.2 | convolution fusion | flops 1197047808 | bytes 14239872 | tf_op jit(solution)/shard_map/dot_general | solution.py:125
  331.4 14.8 %all-gather.2 = f32[256,34]{1,0:T(8,128)} all-gather(f32[32,34]{1,0:T(8,128)S(1)} %fusion.57), channel_id=4, replica_groups=mesh['space'=16,'vel'=8] {'vel'}, dimensions={0}, use_global_device_ids=true | all-gather | bytes 39168 | tf_op jit(solution)/shard_map/all_gather | solution.py:154
  360.2 10.9 %fusion.51 = f32[32,224]{1,0:T(8,128)S(1)} fusion(f32[32,13824]{1,0:T(8,128)S(1)} %fusion.298, f32[32,13824]{1,0:T(8,128)S(1)} %copy-done.5, f32[96,13824]{1,0:T(8,128)S(1)} %bitcast.372, f32[96,13824]{1,0:T(8,128)S(1)} %bitcast.371), kind=kOutput, calls=%fused_computation.73 | convolution fusion | flops 1195285504 | bytes 14184448 | tf_op jit(solution)/shard_map/dot_general | solution.py:57
  371.2 13.1 %all-gather.3 = f32[256,224]{1,0:T(8,128)S(1)} all-gather(f32[32,224]{1,0:T(8,128)S(1)} %fusion.51), channel_id=5, replica_groups=mesh['space'=16,'vel'=8] {'vel'}, dimensions={0}, use_global_device_ids=true | all-gather | bytes 258048 | tf_op jit(solution)/shard_map/all_gather | solution.py:154
  384.3 5.4 collective-permute-start.2
  396.9 7.3 %fusion.38 = f32[32,8192]{1,0:T(8,128)S(1)} fusion(f32[32,8192]{1,0:T(8,128)S(1)} %fusion.293, f32[24,8,64,128]{3,2,1,0:T(8,128)S(1)} %bitcast.368, f32[8192]{0:T(1024)S(1)} %bitcast.401, f32[32]{0:T(128)S(1)} %copy-done.34, f32[8192]{0:T(1024)S(1)} %bitcast.391, f32[32,224]{1,0:T(8,128)S(1)} %reduce_sum.74), kind=kOutput, calls=%fused_computation.44 | convolution fusion | flops 605552640 | bytes 8482944 | tf_op jit(solution)/shard_map/dot_general | solution.py:116
  405.6 6.2 collective-permute-start.4
  418.6 7.3 %fusion.36 = f32[32,8192]{1,0:T(8,128)S(1)} fusion(f32[32,8192]{1,0:T(8,128)S(1)} %fusion.38, f32[24,8,64,128]{3,2,1,0:T(8,128)S(1)} %bitcast.369, f32[8192]{0:T(1024)S(1)} %bitcast.402, f32[32]{0:T(128)S(1)} %copy-done.34, f32[8192]{0:T(1024)S(1)} %bitcast.392, f32[32,224]{1,0:T(8,128)S(1)} %reduce_sum.74), kind=kOutput, calls=%fused_computation.41 | convolution fusion | flops 605552640 | bytes 8482944 | tf_op jit(solution)/shard_map/dot_general | solution.py:116
  427.4 5.6 collective-permute-start.6
  439.2 7.2 %fusion.34 = f32[32,8192]{1,0:T(8,128)S(1)} fusion(f32[32,8192]{1,0:T(8,128)S(1)} %fusion.36, f32[24,8,64,128]{3,2,1,0:T(8,128)S(1)} %bitcast.370, f32[8192]{0:T(1024)S(1)} %bitcast.400, f32[32]{0:T(128)S(1)} %copy-done.34, f32[8192]{0:T(1024)S(1)} %bitcast.393, f32[32,224]{1,0:T(8,128)S(1)} %reduce_sum.74), kind=kOutput, calls=%fused_computation.38 | convolution fusion | flops 605552640 | bytes 8482944 | tf_op jit(solution)/shard_map/dot_general | solution.py:116
  447.4 74.4 %psum.51 = f32[32,32]{0,1:T(8,128)S(1)} all-reduce(f32[32,32]{0,1:T(8,128)S(1)} %convolution_multiply_fusion.2), channel_id=1, replica_groups=mesh['space'=16,'vel'=8] {'space'}, use_global_device_ids=true, to_apply=%region_7.10 | all-reduce | flops 1024 | bytes 8192 | tf_op jit(solution)/shard_map/psum | solution.py:153
  531.4 9.2 %collective-permute-done.7 = f32[32,1,16,128]{3,2,1,0:T(8,128)S(1)} collective-permute-done((f32[32,1,16,128]{3,2,1,0:T(8,128)S(1)}, f32[32,1,16,128]{3,2,1,0:T(8,128)S(1)}, u32[]{:S(2)}, u32[]{:S(2)}) %collective-permute-start.7) | collective-permute-done | bytes 262176 | tf_op jit(solution)/shard_map/ppermute | solution.py:17
  548.5 69.5 %psum.52 = f32[32,160]{1,0:T(8,128)S(1)} all-reduce(f32[32,160]{1,0:T(8,128)S(1)} %convolution_multiply_fusion), channel_id=1, replica_groups=mesh['space'=16,'vel'=8] {'space'}, use_global_device_ids=true, to_apply=%region_8.11 | all-reduce | flops 5120 | bytes 40960 | tf_op jit(solution)/shard_map/psum | solution.py:153
  (282 shorter events, 141.4 us)
Async XLA Ops:
  0.6 236.4 %copy-start = (f32[32,32]{1,0:T(8,128)S(1)}, f32[32,32]{1,0:T(8,128)}, u32[]{:S(2)}) copy-start(f32[32,32]{1,0:T(8,128)} %param.8) | copy-start | bytes 12292
  2.3 154.9 %collective-permute-start = (f32[32,1,16,128]{3,2,1,0:T(8,128)}, f32[32,1,16,128]{3,2,1,0:T(8,128)}, u32[]{:S(2)}, u32[]{:S(2)}) collective-permute-start(f32[32,1,16,128]{3,2,1,0:T(8,128)} %slice.264), channel_id=1, source_target_pairs={{120,0},{0,8},{8,16},{16,24},{24,32},{32,40},{40,48},{48,56},{56,6... | collective-permute-start | bytes 786440 | tf_op jit(solution)/shard_map/ppermute | solution.py:17
  96.8 17.3 %copy-start.36 = (f32[34]{0:T(128)}, f32[34]{0:T(128)S(1)}, u32[]{:S(2)}) copy-start(f32[34]{0:T(128)S(1)} %pad.64.clone) | copy-start | bytes 412
  128.6 30.3 %copy-start.7 = (f32[3,13824]{1,0:T(4,128)}, f32[3,13824]{1,0:T(4,128)S(1)}, u32[]{:S(2)}) copy-start(f32[3,13824]{1,0:T(4,128)S(1)} %get-tuple-element.50) | copy-start | bytes 497668
  130.2 27.0 %copy-start.26 = (f32[32,32]{1,0:T(8,128)S(1)}, f32[32,32]{1,0:T(8,128)}, u32[]{:S(2)}) copy-start(f32[32,32]{1,0:T(8,128)} %copy-done.25) | copy-start | bytes 12292
  160.9 76.5 %copy-start.4 = (f32[32,13824]{1,0:T(8,128)S(1)}, f32[32,13824]{1,0:T(8,128)}, u32[]{:S(2)}) copy-start(f32[32,13824]{1,0:T(8,128)} %copy-done.3) | copy-start | bytes 5308420
  236.3 22.2 %copy-start.21 = (f32[32,160]{1,0:T(8,128)}, f32[32,160]{1,0:T(8,128)S(1)}, u32[]{:S(2)}) copy-start(f32[32,160]{1,0:T(8,128)S(1)} %psum.50) | copy-start | bytes 61444
  258.7 6.7 %copy-start.27 = (f32[32,32]{1,0:T(8,128)S(1)}, f32[32,32]{1,0:T(8,128)}, u32[]{:S(2)}) copy-start(f32[32,32]{1,0:T(8,128)} %get-tuple-element.51) | copy-start | bytes 12292
  266.2 10.7 %copy-start.8 = (f32[3,13824]{1,0:T(4,128)S(1)}, f32[3,13824]{1,0:T(4,128)}, u32[]{:S(2)}) copy-start(f32[3,13824]{1,0:T(4,128)} %copy-done.7) | copy-start | bytes 497668
  276.9 16.7 %copy-start.22 = (f32[32,160]{1,0:T(8,128)S(1)}, f32[32,160]{1,0:T(8,128)}, u32[]{:S(2)}) copy-start(f32[32,160]{1,0:T(8,128)} %copy-done.21) | copy-start | bytes 61444
  276.9 16.9 %copy-start.32 = (f32[32,224]{1,0:T(8,128)S(1)}, f32[32,224]{1,0:T(8,128)}, u32[]{:S(2)}) copy-start(f32[32,224]{1,0:T(8,128)} %concatenate.176) | copy-start | bytes 86020
  320.8 8.6 %copy-start.31 = (f32[1,13824]{1,0:T(1,128)S(1)}, f32[1,13824]{1,0:T(1,128)}, u32[]{:S(2)}) copy-start(f32[1,13824]{1,0:T(1,128)} %copy-done.30) | copy-start | bytes 165892
  320.8 8.6 %copy-start.37 = (f32[34]{0:T(128)S(1)}, f32[34]{0:T(128)}, u32[]{:S(2)}) copy-start(f32[34]{0:T(128)} %copy-done.36) | copy-start | bytes 412
  359.9 30.5 %collective-permute-start.1 = (f32[32,1,16,128]{3,2,1,0:T(8,128)}, f32[32,1,16,128]{3,2,1,0:T(8,128)}, u32[]{:S(2)}, u32[]{:S(2)}) collective-permute-start(f32[32,1,16,128]{3,2,1,0:T(8,128)} %get-tuple-element.48), channel_id=1, source_target_pairs={{0,8},{8,16},{16,24},{24,32},{32,40},{40,48},{48,56},{56,64},{64,7... | collective-permute-start | bytes 786440 | tf_op jit(solution)/shard_map/ppermute | solution.py:27
  360.2 29.5 %copy-start.35 = (f32[32,1]{0,1:T(1,128)S(1)}, f32[32,1]{0,1:T(1,128)}, u32[]{:S(2)}) copy-start(f32[32,1]{0,1:T(1,128)} %convolution_bitcast_fusion.11) | copy-start | bytes 388
  384.3 8.7 %copy-start.15 = (f32[32,4,16,127]{3,2,1,0:T(8,128)S(1)}, f32[32,4,16,127]{3,2,1,0:T(8,128)}, u32[]{:S(2)}) copy-start(f32[32,4,16,127]{3,2,1,0:T(8,128)} %get-tuple-element.40) | copy-start | bytes 3121156
  384.3 8.7 %copy-start.16 = (f32[32,4,16,1]{3,2,1,0:T(8,128)S(1)}, f32[32,4,16,1]{3,2,1,0:T(8,128)}, u32[]{:S(2)}) copy-start(f32[32,4,16,1]{3,2,1,0:T(8,128)} %get-tuple-element.42) | copy-start | bytes 24580
  384.3 11.8 %collective-permute-start.2 = (f32[32,1,16,128]{3,2,1,0:T(8,128)}, f32[32,1,16,128]{3,2,1,0:T(8,128)S(1)}, u32[]{:S(2)}, u32[]{:S(2)}) collective-permute-start(f32[32,1,16,128]{3,2,1,0:T(8,128)} %get-tuple-element.47), channel_id=1, source_target_pairs={{8,0},{16,8},{24,16},{32,24},{40,32},{48,40},{56,48},{64,56},{72,6... | collective-permute-start | bytes 786440 | tf_op jit(solution)/shard_map/ppermute | solution.py:29
  405.5 11.7 %collective-permute-start.3 = (f32[32,1,16,128]{3,2,1,0:T(8,128)S(1)}, f32[32,1,16,128]{3,2,1,0:T(8,128)S(1)}, u32[]{:S(2)}, u32[]{:S(2)}) collective-permute-start(f32[32,1,16,128]{3,2,1,0:T(8,128)S(1)} %get-tuple-element.38), channel_id=1, source_target_pairs={{0,8},{8,16},{16,24},{24,32},{32,40},{40,48},{48,56},{56,64},{64,7... | collective-permute-start | bytes 786440 | tf_op jit(solution)/shard_map/ppermute | solution.py:27
  405.6 12.3 %collective-permute-start.4 = (f32[32,1,16,128]{3,2,1,0:T(8,128)S(1)}, f32[32,1,16,128]{3,2,1,0:T(8,128)S(1)}, u32[]{:S(2)}, u32[]{:S(2)}) collective-permute-start(f32[32,1,16,128]{3,2,1,0:T(8,128)S(1)} %get-tuple-element.37), channel_id=1, source_target_pairs={{8,0},{16,8},{24,16},{32,24},{40,32},{48,40},{56,48},{64,56},{72,6... | collective-permute-start | bytes 786440 | tf_op jit(solution)/shard_map/ppermute | solution.py:29
  427.2 10.5 %collective-permute-start.5 = (f32[32,1,16,128]{3,2,1,0:T(8,128)S(1)}, f32[32,1,16,128]{3,2,1,0:T(8,128)S(1)}, u32[]{:S(2)}, u32[]{:S(2)}) collective-permute-start(f32[32,1,16,128]{3,2,1,0:T(8,128)S(1)} %get-tuple-element.28), channel_id=1, source_target_pairs={{0,8},{8,16},{16,24},{24,32},{32,40},{40,48},{48,56},{56,64},{64,7... | collective-permute-start | bytes 786440 | tf_op jit(solution)/shard_map/ppermute | solution.py:27
  427.4 11.1 %collective-permute-start.6 = (f32[32,1,16,128]{3,2,1,0:T(8,128)S(1)}, f32[32,1,16,128]{3,2,1,0:T(8,128)S(1)}, u32[]{:S(2)}, u32[]{:S(2)}) collective-permute-start(f32[32,1,16,128]{3,2,1,0:T(8,128)S(1)} %get-tuple-element.27), channel_id=1, source_target_pairs={{8,0},{16,8},{24,16},{32,24},{40,32},{48,40},{56,48},{64,56},{72,6... | collective-permute-start | bytes 786440 | tf_op jit(solution)/shard_map/ppermute | solution.py:29
  530.8 9.8 %collective-permute-start.7 = (f32[32,1,16,128]{3,2,1,0:T(8,128)S(1)}, f32[32,1,16,128]{3,2,1,0:T(8,128)S(1)}, u32[]{:S(2)}, u32[]{:S(2)}) collective-permute-start(f32[32,1,16,128]{3,2,1,0:T(8,128)S(1)} %slice.379), channel_id=1, source_target_pairs={{120,0},{0,8},{8,16},{16,24},{24,32},{32,40},{40,48},{48,56},{56,6... | collective-permute-start | bytes 786440 | tf_op jit(solution)/shard_map/ppermute | solution.py:17
  543.4 84.5 %copy-start.1 = (f32[32,32]{1,0:T(8,128)S(1)}, f32[32,32]{1,0:T(8,128)}, u32[]{:S(2)}) copy-start(f32[32,32]{1,0:T(8,128)} %param.8) | copy-start | bytes 12292
  (23 other events, 75.8 us)
